TPU v7x, 512 devices: a whole 4x8x8 slice. The times are simulated.
512 devices in a mesh: gx: 16 (over z, core), gy: 8 (over y), gz: 4 (over x).
Axes of the slice: x: 4, y: 8, z: 8, core: 2. Of those that a mesh axis runs over, the one named last changes fastest.
Arguments:
- snapshot: float32 [512, 1280, 512], P('gx', 'gy', 'gz'), may hold values from -40 to 40
Outputs:
- basis: float32 [512, 128], P('gx')
- core: float32 [128, 1280, 512], P('gx', 'gy', 'gz')
All inputs are finite; a program needn't handle non-finite values.
Results may differ from a plain program's by a relative error of at most 0.0002.
Values sent between devices are 32-bit elements; how exact they have to be, the bound alone decides.
A program may use at most 64 MiB of HBM per device.

v0:
```python
import jax
import jax.numpy as jnp
from jax import lax
from jax.sharding import PartitionSpec as P

RANK = 128
ITERS = 2


def product(left, right):
    return jnp.dot(left, right, precision=lax.Precision.HIGHEST, preferred_element_type=jnp.float32)


def orthonormal(matrix):
    lower = jnp.linalg.cholesky(product(matrix.T, matrix))
    return jax.scipy.linalg.solve_triangular(lower, matrix.T, lower=True).T


def local(snapshot):
    xlocal, ylocal, zlocal = snapshot.shape
    flat = snapshot.reshape(xlocal, ylocal * zlocal)
    fibres = lax.all_to_all(flat, "gx", split_axis=1, concat_axis=0, tiled=True)
    gram = product(fibres, fibres.T)
    factor = jnp.linalg.cholesky(lax.psum(gram, ("gx", "gy", "gz")))
    basis = orthonormal(factor[:, :RANK])
    for step in range(ITERS):
        basis = orthonormal(product(factor, product(factor.T, basis)))
    groups = lax.axis_size("gx")
    own_rows = basis.shape[0] // groups
    mine = lax.dynamic_slice_in_dim(basis, lax.axis_index("gx") * own_rows, own_rows, 0)
    projected = product(basis.T, fibres)
    returned = lax.all_to_all(projected, "gx", split_axis=0, concat_axis=1, tiled=True)
    return (mine, returned.reshape(RANK // groups, ylocal, zlocal))


def solution(mesh):
    in_specs = (P("gx", "gy", "gz"),)
    out_specs = (P("gx", None), P("gx", "gy", "gz"))
    return jax.shard_map(local, mesh=mesh, in_specs=in_specs, out_specs=out_specs, check_vma=False)
```

profile of v0, /device:TPU:1, one launch (start us, length us, event | category | flops | bytes accessed | tf_op | source)
XLA Modules:
  0.0 580.8 jit_solution(15275635226569136335)
XLA Ops:
  7.2 0.0 all-reduce.3.cloned.1.call-start
  7.2 2.6 all_to_all.24
  9.8 1.5 copy.10
  11.3 73.8 %all_to_all.32 = f32[32,16,1280]{2,0,1:T(8,128)S(1)} all-to-all(f32[32,16,1280]{2,0,1:T(8,128)S(1)} %copy.10), channel_id=1, replica_groups=mesh['gx'=16,'gy'=8,'gz'=4] {'gx'}, dimensions={1} | all-to-all | bytes 5242880 | tf_op jit(solution)/shard_map/all_to_all | solution.py:22
  85.1 5.3 fusion.50
  90.5 0.0 all-reduce.3.cloned.1.call-update
  90.5 272.2 %all-reduce.3.cloned.1.call-done = f32[512,512]{0,1:T(8,128)} async-done(((f32[512,512]{0,1:T(8,128)}), f32[512,512]{0,1:T(8,128)}) %all-reduce.3.cloned.1.call-update) | async-done | bytes 1048592 | tf_op jit(solution)/shard_map/psum | solution.py:24
  362.7 2.6 copy.12
  365.2 1.8 fusion
  367.0 1.0 copy-done.3
  368.0 11.7 %cholesky.120 = f32[128,128]{1,0:T(8,128)S(1)} custom-call(f32[128,128]{1,0:T(8,128)S(1)} %cholesky.356), custom_call_target="Cholesky" | custom-call | tf_op jit(solution)/shard_map/jit(cholesky)/cholesky | solution.py:24
  379.8 9.8 %custom-call.32 = f32[1,128,128]{1,2,0:T(8,128)S(1)} custom-call(f32[1,128,128]{2,1,0:T(8,128)S(1)} %get-tuple-element.17), custom_call_target="InvertDiagBlocksLowerTriangular" | custom-call | tf_op jit(solution)/shard_map/jit(cholesky)/cholesky | solution.py:24
  389.6 1.2 cholesky.251
  390.7 2.0 constant_dynamic-update-slice_fusion.2
  392.7 1.2 convolution_subtract_fusion
  394.0 11.9 %cholesky.244 = f32[128,128]{1,0:T(8,128)S(1)} custom-call(f32[128,128]{1,0:T(8,128)S(1)} %cholesky.360), custom_call_target="Cholesky" | custom-call | tf_op jit(solution)/shard_map/jit(cholesky)/cholesky | solution.py:24
  405.9 0.6 fusion.45
  406.5 9.8 %custom-call.33 = f32[1,128,128]{1,2,0:T(8,128)S(1)} custom-call(f32[1,128,128]{2,1,0:T(8,128)S(1)} %get-tuple-element.14), custom_call_target="InvertDiagBlocksLowerTriangular" | custom-call | tf_op jit(solution)/shard_map/jit(cholesky)/cholesky | solution.py:24
  416.3 0.9 convolution_dynamic-update-slice_fusion
  417.3 1.4 convolution_subtract_fusion.1
  418.7 11.7 %cholesky.265 = f32[128,128]{1,0:T(8,128)S(1)} custom-call(f32[128,128]{1,0:T(8,128)S(1)} %cholesky.365), custom_call_target="Cholesky" | custom-call | tf_op jit(solution)/shard_map/jit(cholesky)/cholesky | solution.py:24
  430.4 0.6 fusion.46
  431.1 0.6 compare_reduce_fusion.4
  431.7 10.2 %custom-call.34 = f32[1,128,128]{1,2,0:T(8,128)S(1)} custom-call(f32[1,128,128]{2,1,0:T(8,128)S(1)} %get-tuple-element.11), custom_call_target="InvertDiagBlocksLowerTriangular" | custom-call | tf_op jit(solution)/shard_map/jit(cholesky)/cholesky | solution.py:24
  441.9 0.8 convolution_dynamic-update-slice_fusion.1
  442.7 1.4 convolution_subtract_fusion.2
  444.2 11.7 %cholesky.282 = f32[128,128]{1,0:T(8,128)S(1)} custom-call(f32[128,128]{1,0:T(8,128)S(1)} %convolution_subtract_fusion.2), custom_call_target="Cholesky" | custom-call | tf_op jit(solution)/shard_map/jit(cholesky)/cholesky | solution.py:24
  455.9 0.7 fusion.47
  456.5 0.7 compare_reduce_fusion.3
  457.2 0.6 compare_reduce_fusion.5
  460.5 1.4 select_select_fusion
  461.9 1.0 copy-done
  462.8 0.6 fusion.11
  463.4 0.1 copy.13
  463.5 11.7 %cholesky.325 = f32[128,128]{1,0:T(8,128)S(1)} custom-call(f32[128,128]{1,0:T(8,128)S(1)} %fusion.28), custom_call_target="Cholesky" | custom-call | tf_op jit(solution)/shard_map/jit(cholesky)/cholesky | solution.py:15
  475.3 0.6 compare_reduce_fusion.2
  475.9 0.7 fusion.18
  476.6 9.8 %custom-call.37 = f32[1,128,128]{1,2,0:T(8,128)S(1)} custom-call(f32[1,128,128]{2,1,0:T(8,128)S(1)} %fusion.18), custom_call_target="InvertDiagBlocksLowerTriangular" | custom-call | tf_op jit(solution)/shard_map/jit(_solve_triangular)/triangular_solve | solution.py:16
  486.4 1.5 fusion.8
  487.9 3.2 fusion.51
  491.1 1.0 fusion.52
  492.1 0.6 fusion.53
  492.7 0.1 copy.14
  492.8 11.7 %cholesky.336 = f32[128,128]{1,0:T(8,128)S(1)} custom-call(f32[128,128]{1,0:T(8,128)S(1)} %fusion.26), custom_call_target="Cholesky" | custom-call | tf_op jit(solution)/shard_map/jit(cholesky)/cholesky | solution.py:15
  504.6 0.6 compare_reduce_fusion.1
  505.2 0.7 fusion.19
  505.9 9.8 %custom-call.38 = f32[1,128,128]{1,2,0:T(8,128)S(1)} custom-call(f32[1,128,128]{2,1,0:T(8,128)S(1)} %fusion.19), custom_call_target="InvertDiagBlocksLowerTriangular" | custom-call | tf_op jit(solution)/shard_map/jit(_solve_triangular)/triangular_solve | solution.py:16
  515.7 0.4 fusion.6
  516.1 3.0 fusion.54
  519.2 1.0 fusion.55
  520.1 0.8 fusion.56
  520.9 0.1 copy.15
  521.1 11.7 %cholesky.347 = f32[128,128]{1,0:T(8,128)S(1)} custom-call(f32[128,128]{1,0:T(8,128)S(1)} %fusion.24), custom_call_target="Cholesky" | custom-call | tf_op jit(solution)/shard_map/jit(cholesky)/cholesky | solution.py:15
  532.8 0.6 compare_reduce_fusion
  533.5 0.7 fusion.20
  534.1 9.8 %custom-call.39 = f32[1,128,128]{1,2,0:T(8,128)S(1)} custom-call(f32[1,128,128]{2,1,0:T(8,128)S(1)} %fusion.20), custom_call_target="InvertDiagBlocksLowerTriangular" | custom-call | tf_op jit(solution)/shard_map/jit(_solve_triangular)/triangular_solve | solution.py:16
  543.9 0.4 fusion.4
  544.4 2.3 fusion.2
  546.6 6.0 %all-to-all-start.1 = ((f32[16,8,1280]{2,1,0:T(8,128)}), f32[16,8,1280]{2,1,0:T(8,128)S(1)}, u32[]{:S(2)}, u32[]{:S(2)}) async-start(f32[16,8,1280]{2,1,0:T(8,128)} %fusion.2), calls=%async_computation.1 | async-start | bytes 1310720 | tf_op jit(solution)/shard_map/all_to_all | solution.py:32
  552.7 0.1 dynamic-slice_bitcast_fusion
  552.8 0.7 copy.17
  553.4 19.2 %all-to-all-done.1 = f32[16,8,1280]{2,1,0:T(8,128)S(1)} async-done(((f32[16,8,1280]{2,1,0:T(8,128)}), f32[16,8,1280]{2,1,0:T(8,128)S(1)}, u32[]{:S(2)}, u32[]{:S(2)}) %all-to-all-start.1) | async-done | bytes 655392 | tf_op jit(solution)/shard_map/all_to_all | solution.py:32
  572.6 0.2 copy.16
  572.8 0.9 reshape.52
  (16 shorter events, 0.2 us)
Async XLA Ops:
  7.2 355.5 %all-reduce.3.cloned.1.call-start = ((), (), s32[]{:S(2)}) async-start(), calls=%async_computation.2 | async-start | bytes 2097152 | tf_op jit(solution)/shard_map/psum | solution.py:24
  367.0 1.0 copy-start.3
  461.8 1.0 copy-start
  486.4 4.7 copy-start.1
  515.7 3.5 copy-start.2
  546.6 26.0 %all-to-all-start.1 = ((f32[16,8,1280]{2,1,0:T(8,128)}), f32[16,8,1280]{2,1,0:T(8,128)S(1)}, u32[]{:S(2)}, u32[]{:S(2)}) async-start(f32[16,8,1280]{2,1,0:T(8,128)} %fusion.2), calls=%async_computation.1 | async-start | bytes 1310720 | tf_op jit(solution)/shard_map/all_to_all | solution.py:32
Sparse Core Ops, SparseCore 0:
  90.6 272.0 all-reduce.2
where the time goes:
time: 584 us; the launch traced here: 581 us
  waiting for transfers between devices  291 us (50%)
  other arithmetic  153 us (26%)
  blocking collectives  73.8 us (13%)
  matrix products  27.9 us (5%)
  between operations  17.2 us (3%)
  local copies, waits for them, and re-layouts  12 us (2%)
  starting transfers between devices  6.08 us (1%)
    psum x1, waiting for transfers between devices, local(): factor = jnp.linalg.cholesky(lax.psum(gram, ('gx', 'gy', 'gz')))  272 us
    another operation x14, other arithmetic, local(): factor = jnp.linalg.cholesky(lax.psum(gram, ('gx', 'gy', 'gz')))  80.8 us
    all_to_all x1, blocking collectives, local(): fibres = lax.all_to_all(flat, 'gx', split_axis=1, concat_axis=0, tiled=True)  73.8 us
    another operation x9, other arithmetic, orthonormal(): lower = jnp.linalg.cholesky(product(matrix.T, matrix))  37.2 us
    another operation x6, other arithmetic, orthonormal(): return jax.scipy.linalg.solve_triangular(lower, matrix.T, lower=True).T  31.4 us
    all_to_all x1, waiting for transfers between devices, local(): lax.all_to_all(projected, 'gx', split_axis=0, concat_axis=1, tiled=True)  19.2 us
    dot_general x9, matrix products, product(): jnp.dot(left, right, precision=lax.Precision.HIGHEST, preferred_element_t...  17.8 us
  transfers between devices with their start and end apart: 2, of which 2 were waited for; matrix products, arithmetic and copies ran while one was open for 0% of the time, Pallas kernels for 0%

commit v1 on v0

--- a/solution.py
+++ b/solution.py
@@ -5,6 +5,18 @@
 
 RANK = 128
 ITERS = 2
+
+
+def treat_the_limits(here_x, dev_axis):
+    return jnp.concatenate(
+        lax.all_to_all(
+            jnp.stack(jnp.split(here_x, lax.axis_size(dev_axis), axis=1)),
+            dev_axis,
+            split_axis=0,
+            concat_axis=0,
+        ),
+        axis=0,
+    )
 
 
 def product(left, right):
@@ -19,7 +31,7 @@
 def local(snapshot):
     xlocal, ylocal, zlocal = snapshot.shape
     flat = snapshot.reshape(xlocal, ylocal * zlocal)
-    fibres = lax.all_to_all(flat, "gx", split_axis=1, concat_axis=0, tiled=True)
+    fibres = treat_the_limits(flat, "gx")
     gram = product(fibres, fibres.T)
     factor = jnp.linalg.cholesky(lax.psum(gram, ("gx", "gy", "gz")))
     basis = orthonormal(factor[:, :RANK])

time: 584 us -> 583 us (level)
  no operation moved by 1% of the time
where the time goes in v1:
time: 583 us; the launch traced here: 580 us
  waiting for transfers between devices  291 us (50%)
  other arithmetic  153 us (26%)
  blocking collectives  73.8 us (13%)
  matrix products  27.9 us (5%)
  between operations  17.3 us (3%)
  local copies, waits for them, and re-layouts  11.4 us (2%)
  starting transfers between devices  6.06 us (1%)
    psum x1, waiting for transfers between devices, local(): factor = jnp.linalg.cholesky(lax.psum(gram, ('gx', 'gy', 'gz')))  272 us
    another operation x14, other arithmetic, local(): factor = jnp.linalg.cholesky(lax.psum(gram, ('gx', 'gy', 'gz')))  80.8 us
    all_to_all x1, blocking collectives, treat_the_limits(): lax.all_to_all(jnp.stack(jnp.split(here_x, lax.axis_size(dev_axis), axis=...  73.8 us
    another operation x9, other arithmetic, orthonormal(): lower = jnp.linalg.cholesky(product(matrix.T, matrix))  37.2 us
    another operation x6, other arithmetic, orthonormal(): return jax.scipy.linalg.solve_triangular(lower, matrix.T, lower=True).T  31.4 us
    all_to_all x1, waiting for transfers between devices, local(): lax.all_to_all(projected, 'gx', split_axis=0, concat_axis=1, tiled=True)  19.2 us
    dot_general x9, matrix products, product(): jnp.dot(left, right, precision=lax.Precision.HIGHEST, preferred_element_t...  17.8 us
  transfers between devices with their start and end apart: 2, of which 2 were waited for; matrix products, arithmetic and copies ran while one was open for 0% of the time, Pallas kernels for 0%

profile of v1, /device:TPU:1, one launch (start us, length us, event | category | flops | bytes accessed | tf_op | source)
XLA Modules:
  0.0 580.3 jit_solution(9135855639951845390)
XLA Ops:
  7.2 0.0 all-reduce.3.cloned.1.call-start
  7.2 3.3 copy.19
  10.8 73.8 %all_to_all.18 = f32[16,32,1280]{2,1,0:T(8,128)S(1)} all-to-all(f32[16,32,1280]{2,1,0:T(8,128)S(1)} %fusion.16), channel_id=1, replica_groups=mesh['gx'=16,'gy'=8,'gz'=4] {'gx'}, dimensions={0} | all-to-all | bytes 5242880 | tf_op jit(solution)/shard_map/all_to_all | solution.py:12
  84.6 5.3 fusion.66
  89.9 0.0 all-reduce.3.cloned.1.call-update
  89.9 272.3 %all-reduce.3.cloned.1.call-done = f32[512,512]{0,1:T(8,128)} async-done(((f32[512,512]{0,1:T(8,128)}), f32[512,512]{0,1:T(8,128)}) %all-reduce.3.cloned.1.call-update) | async-done | bytes 1048592 | tf_op jit(solution)/shard_map/psum | solution.py:36
  362.2 2.6 copy.10
  364.8 1.8 fusion
  366.6 0.0 copy-start.3
  366.6 1.0 copy-done.3
  367.6 11.7 %cholesky.120 = f32[128,128]{1,0:T(8,128)S(1)} custom-call(f32[128,128]{1,0:T(8,128)S(1)} %cholesky.356), custom_call_target="Cholesky" | custom-call | tf_op jit(solution)/shard_map/jit(cholesky)/cholesky | solution.py:36
  379.3 1.2 cholesky.251
  380.5 9.8 %custom-call.32 = f32[1,128,128]{1,2,0:T(8,128)S(1)} custom-call(f32[1,128,128]{2,1,0:T(8,128)S(1)} %get-tuple-element.17), custom_call_target="InvertDiagBlocksLowerTriangular" | custom-call | tf_op jit(solution)/shard_map/jit(cholesky)/cholesky | solution.py:36
  390.3 2.0 constant_dynamic-update-slice_fusion.2
  392.3 1.3 convolution_subtract_fusion
  393.5 11.9 %cholesky.244 = f32[128,128]{1,0:T(8,128)S(1)} custom-call(f32[128,128]{1,0:T(8,128)S(1)} %cholesky.360), custom_call_target="Cholesky" | custom-call | tf_op jit(solution)/shard_map/jit(cholesky)/cholesky | solution.py:36
  405.4 0.6 fusion.61
  406.1 9.8 %custom-call.33 = f32[1,128,128]{1,2,0:T(8,128)S(1)} custom-call(f32[1,128,128]{2,1,0:T(8,128)S(1)} %get-tuple-element.14), custom_call_target="InvertDiagBlocksLowerTriangular" | custom-call | tf_op jit(solution)/shard_map/jit(cholesky)/cholesky | solution.py:36
  415.9 0.9 convolution_dynamic-update-slice_fusion
  416.8 1.4 convolution_subtract_fusion.1
  418.3 11.7 %cholesky.265 = f32[128,128]{1,0:T(8,128)S(1)} custom-call(f32[128,128]{1,0:T(8,128)S(1)} %cholesky.365), custom_call_target="Cholesky" | custom-call | tf_op jit(solution)/shard_map/jit(cholesky)/cholesky | solution.py:36
  430.0 0.6 fusion.62
  430.6 0.6 compare_reduce_fusion.4
  431.3 10.2 %custom-call.34 = f32[1,128,128]{1,2,0:T(8,128)S(1)} custom-call(f32[1,128,128]{2,1,0:T(8,128)S(1)} %get-tuple-element.11), custom_call_target="InvertDiagBlocksLowerTriangular" | custom-call | tf_op jit(solution)/shard_map/jit(cholesky)/cholesky | solution.py:36
  441.4 0.8 convolution_dynamic-update-slice_fusion.1
  442.3 1.4 convolution_subtract_fusion.2
  443.7 11.7 %cholesky.282 = f32[128,128]{1,0:T(8,128)S(1)} custom-call(f32[128,128]{1,0:T(8,128)S(1)} %convolution_subtract_fusion.2), custom_call_target="Cholesky" | custom-call | tf_op jit(solution)/shard_map/jit(cholesky)/cholesky | solution.py:36
  455.4 0.7 fusion.63
  456.1 0.7 compare_reduce_fusion.3
  456.8 0.6 compare_reduce_fusion.5
  460.0 1.4 select_select_fusion
  461.4 1.0 copy-done
  462.4 0.6 fusion.11
  463.0 0.1 copy.11
  463.1 11.7 %cholesky.325 = f32[128,128]{1,0:T(8,128)S(1)} custom-call(f32[128,128]{1,0:T(8,128)S(1)} %fusion.44), custom_call_target="Cholesky" | custom-call | tf_op jit(solution)/shard_map/jit(cholesky)/cholesky | solution.py:27
  474.8 0.6 compare_reduce_fusion.2
  475.5 0.7 fusion.34
  476.2 9.8 %custom-call.37 = f32[1,128,128]{1,2,0:T(8,128)S(1)} custom-call(f32[1,128,128]{2,1,0:T(8,128)S(1)} %fusion.34), custom_call_target="InvertDiagBlocksLowerTriangular" | custom-call | tf_op jit(solution)/shard_map/jit(_solve_triangular)/triangular_solve | solution.py:28
  486.0 1.5 fusion.8
  487.4 3.2 fusion.67
  490.7 1.0 fusion.68
  491.6 0.6 fusion.69
  492.2 0.1 copy.12
  492.4 11.7 %cholesky.336 = f32[128,128]{1,0:T(8,128)S(1)} custom-call(f32[128,128]{1,0:T(8,128)S(1)} %fusion.42), custom_call_target="Cholesky" | custom-call | tf_op jit(solution)/shard_map/jit(cholesky)/cholesky | solution.py:27
  504.1 0.6 compare_reduce_fusion.1
  504.7 0.7 fusion.35
  505.4 9.8 %custom-call.38 = f32[1,128,128]{1,2,0:T(8,128)S(1)} custom-call(f32[1,128,128]{2,1,0:T(8,128)S(1)} %fusion.35), custom_call_target="InvertDiagBlocksLowerTriangular" | custom-call | tf_op jit(solution)/shard_map/jit(_solve_triangular)/triangular_solve | solution.py:28
  515.2 0.4 fusion.6
  515.7 3.0 fusion.70
  518.7 1.0 fusion.71
  519.7 0.8 fusion.72
  520.5 0.1 copy.13
  520.6 11.7 %cholesky.347 = f32[128,128]{1,0:T(8,128)S(1)} custom-call(f32[128,128]{1,0:T(8,128)S(1)} %fusion.40), custom_call_target="Cholesky" | custom-call | tf_op jit(solution)/shard_map/jit(cholesky)/cholesky | solution.py:27
  532.4 0.6 compare_reduce_fusion
  533.0 0.7 fusion.36
  533.7 9.8 %custom-call.39 = f32[1,128,128]{1,2,0:T(8,128)S(1)} custom-call(f32[1,128,128]{2,1,0:T(8,128)S(1)} %fusion.36), custom_call_target="InvertDiagBlocksLowerTriangular" | custom-call | tf_op jit(solution)/shard_map/jit(_solve_triangular)/triangular_solve | solution.py:28
  543.5 0.4 fusion.4
  543.9 2.3 fusion.2
  546.2 6.0 %all-to-all-start.1 = ((f32[16,8,1280]{2,1,0:T(8,128)}), f32[16,8,1280]{2,1,0:T(8,128)S(1)}, u32[]{:S(2)}, u32[]{:S(2)}) async-start(f32[16,8,1280]{2,1,0:T(8,128)} %fusion.2), calls=%async_computation.1 | async-start | bytes 1310720 | tf_op jit(solution)/shard_map/all_to_all | solution.py:44
  552.2 0.1 dynamic-slice_bitcast_fusion
  552.3 0.7 copy.15
  553.0 19.2 %all-to-all-done.1 = f32[16,8,1280]{2,1,0:T(8,128)S(1)} async-done(((f32[16,8,1280]{2,1,0:T(8,128)}), f32[16,8,1280]{2,1,0:T(8,128)S(1)}, u32[]{:S(2)}, u32[]{:S(2)}) %all-to-all-start.1) | async-done | bytes 655392 | tf_op jit(solution)/shard_map/all_to_all | solution.py:44
  572.2 0.2 copy.14
  572.4 0.9 reshape.55
  (31 shorter events, 0.4 us)
Async XLA Ops:
  7.2 355.0 %all-reduce.3.cloned.1.call-start = ((), (), s32[]{:S(2)}) async-start(), calls=%async_computation.2 | async-start | bytes 2097152 | tf_op jit(solution)/shard_map/psum | solution.py:36
  366.6 1.0 copy-start.3
  461.4 1.0 copy-start
  486.0 4.7 copy-start.1
  515.2 3.5 copy-start.2
  546.2 26.0 %all-to-all-start.1 = ((f32[16,8,1280]{2,1,0:T(8,128)}), f32[16,8,1280]{2,1,0:T(8,128)S(1)}, u32[]{:S(2)}, u32[]{:S(2)}) async-start(f32[16,8,1280]{2,1,0:T(8,128)} %fusion.2), calls=%async_computation.1 | async-start | bytes 1310720 | tf_op jit(solution)/shard_map/all_to_all | solution.py:44
Sparse Core Ops, SparseCore 0:
  90.1 272.0 all-reduce.2
